TPU v7x, 256 devices: a whole 4x4x8 slice. The times are simulated.
256 devices in a mesh: dp: 16 (over y, x), expert: 16 (over z, core).
Axes of the slice: x: 4, y: 4, z: 8, core: 2. Of those that a mesh axis runs over, the one named last changes fastest.
Arguments:
- tokens: bfloat16 [16384, 2048], P(('dp', 'expert')), may hold values from -6 to 6
- expert_ids: int32 [16384, 8], P(('dp', 'expert')), may hold values from 0 to 127, all different within a row; in each aligned block of 32 rows (0 to 31, 32 to 63, ...) at most 3 rows name the same one
- gate_fixed: int32 [16384, 8], P(('dp', 'expert')), may hold values from 1 to 65535
- w_gate: bfloat16 [256, 2048, 384], P(('dp', 'expert')), may hold values from -0.125 to 0.125
- w_up: bfloat16 [256, 2048, 384], P(('dp', 'expert')), may hold values from -0.125 to 0.125
- w_down: bfloat16 [256, 384, 2048], P(('dp', 'expert')), may hold values from -0.21875 to 0.21875
Outputs:
- mixed: float32 [16384, 2048], P(('dp', 'expert'))
Inputs may be any that keep to these rules, and one draw needn't show every extreme that they name: `expert_ids`: each row names 8 different experts. In each aligned block of 32 rows (the first or the second half of one device's rows) no expert is named by more than 3 rows, a bound that some block reaches.
All inputs are finite; a program needn't handle non-finite values.
Results may differ from a plain program's by a relative error of at most 0.0041.
Values may be sent and summed in bfloat16 or wider, within the bound.
No kernel may reach another device: no remote copies, remote signals or barrier semaphores. Data moves between devices by JAX's collectives and lax.ppermute only.
A program may use at most 64 MiB of HBM per device.

v0:
```python
import jax
import jax.numpy as jnp
from jax import lax
from jax.sharding import PartitionSpec as P


def partner(x, axis, stride):
    return lax.ppermute(x, axis, [(i, i ^ 1 << stride) for i in range(lax.axis_size(axis))])


def per_device(tokens, expert_ids, gate_fixed, w_gate, w_up, w_down):
    dp_count = lax.axis_size("dp")
    col_count = lax.axis_size("expert")
    pair_count = col_count // 2
    dev_count = dp_count * col_count
    expert_count = dev_count // 2
    token_count, width = tokens.shape
    choice_count = expert_ids.shape[1]
    capacity = 3 * token_count * choice_count // (4 * expert_count)
    half_rows = token_count // 2
    other_gate, other_up, other_down = partner((w_gate[0], w_up[0], w_down[0]), "expert", 0)
    gate_full = jnp.concatenate([w_gate[0], other_gate], axis=1)
    up_full = jnp.concatenate([w_up[0], other_up], axis=1)
    down_full = jnp.concatenate([w_down[0], other_down], axis=0)
    gates = gate_fixed.astype(jnp.float32)
    mix_weight = gates / jnp.sum(gates, axis=1, keepdims=True)
    flat_ids = expert_ids.reshape(-1)
    choice_pos = jnp.arange(token_count * choice_count, dtype=jnp.int32)
    half_index = choice_pos // choice_count // half_rows
    onehot = (flat_ids[:, None] == jnp.arange(expert_count, dtype=jnp.int32)[None, :]).astype(
        jnp.int32
    )
    onehot = onehot.reshape(2, half_rows * choice_count, expert_count)
    earlier = jnp.cumsum(onehot, axis=1) - onehot
    slot_index = jnp.sum(earlier * onehot, axis=2).reshape(-1)
    dest_dp = flat_ids // pair_count
    dest_col = 2 * (flat_ids % pair_count) + half_index
    target = (dest_dp * col_count + dest_col) * capacity + slot_index
    repeated = jnp.repeat(tokens, choice_count, axis=0)
    outgoing = jnp.zeros((dev_count * capacity, width), jnp.bfloat16).at[target].set(repeated)
    outgoing = outgoing.reshape(dp_count, col_count, capacity, width)
    first_section = lax.all_to_all(outgoing, "dp", split_axis=0, concat_axis=0, tiled=True)
    arrived = lax.all_to_all(first_section, "expert", split_axis=1, concat_axis=1, tiled=True)
    shape_in = arrived.shape
    token_rows = arrived.reshape(-1, width)
    gate_part = jnp.dot(token_rows, gate_full, preferred_element_type=jnp.float32)
    up_part = jnp.dot(token_rows, up_full, preferred_element_type=jnp.float32)
    hidden = (jax.nn.silu(gate_part) * up_part).astype(jnp.bfloat16)
    expert_out = jnp.dot(hidden, down_full, preferred_element_type=jnp.float32).astype(jnp.bfloat16)
    returned = lax.all_to_all(
        expert_out.reshape(shape_in), "expert", split_axis=1, concat_axis=1, tiled=True
    )
    home = lax.all_to_all(returned, "dp", split_axis=0, concat_axis=0, tiled=True)
    home_flat = home.reshape(dev_count * capacity, width)
    picked = home_flat[target].reshape(token_count, choice_count, width)
    mixed = jnp.sum(picked.astype(jnp.float32) * mix_weight[:, :, None], axis=1)
    return mixed


def solution(mesh):
    placed = (
        P(("dp", "expert"), None),
        P(("dp", "expert"), None),
        P(("dp", "expert"), None),
        P(("dp", "expert"), None, None),
        P(("dp", "expert"), None, None),
        P(("dp", "expert"), None, None),
    )
    return jax.shard_map(
        per_device, mesh=mesh, in_specs=placed, out_specs=P(("dp", "expert"), None), check_vma=False
    )
```

profile of v0, /device:TPU:1, one launch (start us, length us, event | category | flops | bytes accessed | tf_op | source)
XLA Modules:
  0.0 335.0 jit_solution(7348025419594827379)
XLA Ops:
  0.0 0.8 copy.14
  1.2 0.4 fusion.17
  2.2 4.6 %scatter_custom_fusion = bf16[768,2048]{1,0:T(8,128)(2,1)S(1)} fusion(s32[512]{0:T(512)S(1)} %bitcast.27, bf16[]{:T(256)} %constant.54.clone.1, bf16[64,2048]{1,0:T(8,128)(2,1)S(1)} %copy-done), kind=kCustom, calls=%fused_computation.17 | custom fusion | bytes 3407874 | tf_op jit(solution)/shard_map/scatter | solution.py:40
  6.8 4.4 %reshape.259 = bf16[16,16,3,2048]{3,2,1,0:T(4,128)(2,1)} reshape(bf16[768,2048]{1,0:T(8,128)(2,1)S(1)} %scatter_custom_fusion) | data formatting | bytes 6291456 | tf_op jit(solution)/shard_map/reshape | solution.py:41
  11.2 4.7 %copy.19 = bf16[16,16,3,2048]{3,1,2,0:T(8,128)(2,1)S(1)} copy(bf16[16,16,3,2048]{3,2,1,0:T(4,128)(2,1)} %reshape.259) | data formatting | bytes 6291456 | tf_op jit(solution)/shard_map/reshape | solution.py:41
  15.9 46.0 %all_to_all.20 = bf16[16,16,3,2048]{3,1,2,0:T(8,128)(2,1)S(1)} all-to-all(bf16[16,16,3,2048]{3,1,2,0:T(8,128)(2,1)S(1)} %copy.19), channel_id=1, replica_groups=mesh['dp'=16,'expert'=16] {'dp'}, dimensions={0} | all-to-all | bytes 6291456 | tf_op jit(solution)/shard_map/all_to_all | solution.py:42
  61.9 3.4 %copy.20 = bf16[16,16,3,2048]{3,0,2,1:T(8,128)(2,1)} copy(bf16[16,16,3,2048]{3,1,2,0:T(8,128)(2,1)S(1)} %all_to_all.20) | data formatting | bytes 6291456 | tf_op jit(solution)/shard_map/all_to_all | solution.py:42
  65.3 10.5 %all-to-all-start.1 = ((bf16[16,16,3,2048]{3,0,2,1:T(8,128)(2,1)}), bf16[16,16,3,2048]{3,0,2,1:T(8,128)(2,1)S(1)}, u32[]{:S(2)}, u32[]{:S(2)}) async-start(bf16[16,16,3,2048]{3,0,2,1:T(8,128)(2,1)} %copy.20), calls=%async_computation.1 | async-start | bytes 6291456 | tf_op jit(solution)/shard_map/all_to_all | solution.py:43
  76.5 70.3 %all-to-all-done.1 = bf16[16,16,3,2048]{3,0,2,1:T(8,128)(2,1)S(1)} async-done(((bf16[16,16,3,2048]{3,0,2,1:T(8,128)(2,1)}), bf16[16,16,3,2048]{3,0,2,1:T(8,128)(2,1)S(1)}, u32[]{:S(2)}, u32[]{:S(2)}) %all-to-all-start.1) | async-done | bytes 3145760 | tf_op jit(solution)/shard_map/all_to_all | solution.py:43
  146.8 4.6 %copy.21 = bf16[16,16,3,2048]{3,2,1,0:T(4,128)(2,1)} copy(bf16[16,16,3,2048]{3,0,2,1:T(8,128)(2,1)S(1)} %all-to-all-done.1) | data formatting | bytes 6291456 | tf_op jit(solution)/shard_map/all_to_all | solution.py:43
  151.4 7.5 %reshape.260 = bf16[768,2048]{1,0:T(8,128)(2,1)S(1)} reshape(bf16[16,16,3,2048]{3,2,1,0:T(4,128)(2,1)} %copy.21) | data formatting | bytes 6291456 | tf_op jit(solution)/shard_map/reshape | solution.py:45
  158.9 4.6 %fusion.1 = f32[768,768]{1,0:T(8,128)S(1)} fusion(bf16[768,2048]{1,0:T(8,128)(2,1)S(1)} %reshape.260, bf16[2048,384]{1,0:T(8,128)(2,1)} %collective-permute-done, bf16[2048,384]{1,0:T(8,128)(2,1)} %bitcast.31), kind=kOutput, calls=%fused_computation.5 | convolution fusion | flops 2422210560 | bytes 8650752 | tf_op jit(solution)/shard_map/dot_general | solution.py:46
  163.5 4.1 %fusion.5 = f32[768,768]{1,0:T(8,128)S(1)} fusion(bf16[768,2048]{1,0:T(8,128)(2,1)S(1)} %reshape.260, bf16[2048,384]{1,0:T(8,128)(2,1)} %collective-permute-done.1, bf16[2048,384]{1,0:T(8,128)(2,1)S(1)} %bitcast.33), kind=kOutput, calls=%fused_computation.9 | convolution fusion | flops 2422210560 | bytes 8650752 | tf_op jit(solution)/shard_map/dot_general | solution.py:47
  167.7 4.1 %convolution_convert_fusion = bf16[768,2048]{1,0:T(8,128)(2,1)S(1)} fusion(bf16[384,2048]{1,0:T(8,128)(2,1)} %collective-permute-done.2, bf16[384,2048]{1,0:T(8,128)(2,1)S(1)} %bitcast.35, f32[768,768]{1,0:T(8,128)S(1)} %fusion.5, f32[768,768]{1,0:T(8,128)S(1)} %fusion.1), kind=kOutput, calls=%fused_computation.4 | convolution fusion | flops 2427322368 | bytes 11010048 | tf_op jit(solution)/shard_map/dot_general | solution.py:49
  171.8 4.4 %reshape.261 = bf16[16,16,3,2048]{3,2,1,0:T(4,128)(2,1)} reshape(bf16[768,2048]{1,0:T(8,128)(2,1)S(1)} %convolution_convert_fusion) | data formatting | bytes 6291456 | tf_op jit(solution)/shard_map/reshape | solution.py:51
  176.2 4.7 %copy.22 = bf16[16,16,3,2048]{3,0,2,1:T(8,128)(2,1)S(1)} copy(bf16[16,16,3,2048]{3,2,1,0:T(4,128)(2,1)} %reshape.261) | data formatting | bytes 6291456 | tf_op jit(solution)/shard_map/reshape | solution.py:51
  180.9 78.7 %all_to_all.21 = bf16[16,16,3,2048]{3,0,2,1:T(8,128)(2,1)S(1)} all-to-all(bf16[16,16,3,2048]{3,0,2,1:T(8,128)(2,1)S(1)} %copy.22), channel_id=1, replica_groups=mesh['dp'=16,'expert'=16] {'expert'}, dimensions={1} | all-to-all | bytes 6291456 | tf_op jit(solution)/shard_map/all_to_all | solution.py:50
  259.6 3.4 %copy.23 = bf16[16,16,3,2048]{3,1,2,0:T(8,128)(2,1)} copy(bf16[16,16,3,2048]{3,0,2,1:T(8,128)(2,1)S(1)} %all_to_all.21) | data formatting | bytes 6291456 | tf_op jit(solution)/shard_map/all_to_all | solution.py:50
  263.0 4.1 %all-to-all-start.3 = ((bf16[16,16,3,2048]{3,1,2,0:T(8,128)(2,1)}), bf16[16,16,3,2048]{3,1,2,0:T(8,128)(2,1)S(1)}, u32[]{:S(2)}, u32[]{:S(2)}) async-start(bf16[16,16,3,2048]{3,1,2,0:T(8,128)(2,1)} %copy.23), calls=%async_computation.3 | async-start | bytes 6291456 | tf_op jit(solution)/shard_map/all_to_all | solution.py:53
  267.3 47.9 %all-to-all-done.3 = bf16[16,16,3,2048]{3,1,2,0:T(8,128)(2,1)S(1)} async-done(((bf16[16,16,3,2048]{3,1,2,0:T(8,128)(2,1)}), bf16[16,16,3,2048]{3,1,2,0:T(8,128)(2,1)S(1)}, u32[]{:S(2)}, u32[]{:S(2)}) %all-to-all-start.3) | async-done | bytes 3145760 | tf_op jit(solution)/shard_map/all_to_all | solution.py:53
  315.2 4.7 %copy.24 = bf16[16,16,3,2048]{3,2,1,0:T(4,128)(2,1)} copy(bf16[16,16,3,2048]{3,1,2,0:T(8,128)(2,1)S(1)} %all-to-all-done.3) | data formatting | bytes 6291456 | tf_op jit(solution)/shard_map/all_to_all | solution.py:53
  319.9 7.5 %reshape.262 = bf16[768,2048]{1,0:T(8,128)(2,1)S(1)} reshape(bf16[16,16,3,2048]{3,2,1,0:T(4,128)(2,1)} %copy.24) | data formatting | bytes 6291456 | tf_op jit(solution)/shard_map/reshape | solution.py:54
  327.4 3.3 gather_fusion
  330.7 4.2 %fusion = f32[64,2048]{1,0:T(8,128)} fusion(bf16[512,2048]{1,0:T(8,128)(2,1)} %gather_fusion, f32[64,8]{1,0:T(8,128)S(1)} %copy.25), kind=kLoop, calls=%fused_computation.3 | loop fusion | flops 3014656 | bytes 2623488 | tf_op jit(solution)/shard_map/reduce_sum | solution.py:56
  (32 shorter events, 1.7 us)
Async XLA Ops:
  0.0 2.2 copy-start
  65.3 81.4 %all-to-all-start.1 = ((bf16[16,16,3,2048]{3,0,2,1:T(8,128)(2,1)}), bf16[16,16,3,2048]{3,0,2,1:T(8,128)(2,1)S(1)}, u32[]{:S(2)}, u32[]{:S(2)}) async-start(bf16[16,16,3,2048]{3,0,2,1:T(8,128)(2,1)} %copy.20), calls=%async_computation.1 | async-start | bytes 6291456 | tf_op jit(solution)/shard_map/all_to_all | solution.py:43
  75.8 83.1 %collective-permute-start = (bf16[2048,384]{1,0:T(8,128)(2,1)}, bf16[2048,384]{1,0:T(8,128)(2,1)}, u32[]{:S(2)}, u32[]{:S(2)}) collective-permute-start(bf16[2048,384]{1,0:T(8,128)(2,1)} %bitcast.30), channel_id=1, source_target_pairs={{0,1},{1,0},{2,3},{3,2},{4,5},{5,4},{6,7},{7,6},{8,9},{9,8},{10,11... | collective-permute-start | bytes 4718600 | tf_op jit(solution)/shard_map/ppermute | solution.py:8
  76.0 87.6 %collective-permute-start.1 = (bf16[2048,384]{1,0:T(8,128)(2,1)}, bf16[2048,384]{1,0:T(8,128)(2,1)}, u32[]{:S(2)}, u32[]{:S(2)}) collective-permute-start(bf16[2048,384]{1,0:T(8,128)(2,1)} %bitcast.32), channel_id=1, source_target_pairs={{0,1},{1,0},{2,3},{3,2},{4,5},{5,4},{6,7},{7,6},{8,9},{9,8},{10,11... | collective-permute-start | bytes 4718600 | tf_op jit(solution)/shard_map/ppermute | solution.py:8
  76.3 91.4 %collective-permute-start.2 = (bf16[384,2048]{1,0:T(8,128)(2,1)}, bf16[384,2048]{1,0:T(8,128)(2,1)}, u32[]{:S(2)}, u32[]{:S(2)}) collective-permute-start(bf16[384,2048]{1,0:T(8,128)(2,1)} %bitcast.34), channel_id=1, source_target_pairs={{0,1},{1,0},{2,3},{3,2},{4,5},{5,4},{6,7},{7,6},{8,9},{9,8},{10,11... | collective-permute-start | bytes 4718600 | tf_op jit(solution)/shard_map/ppermute | solution.py:8
  158.9 4.6 %copy-start.3 = (bf16[1,2048,384]{2,1,0:T(8,128)(2,1)S(1)}, bf16[1,2048,384]{2,1,0:T(8,128)(2,1)}, u32[]{:S(2)}) copy-start(bf16[1,2048,384]{2,1,0:T(8,128)(2,1)} %param.10) | copy-start | bytes 4718596
  163.5 4.2 %copy-start.4 = (bf16[1,384,2048]{2,1,0:T(8,128)(2,1)S(1)}, bf16[1,384,2048]{2,1,0:T(8,128)(2,1)}, u32[]{:S(2)}) copy-start(bf16[1,384,2048]{2,1,0:T(8,128)(2,1)} %param.11) | copy-start | bytes 4718596
  263.0 4.1 %copy-start.2 = (s32[64,8]{0,1:T(8,128)S(1)}, s32[64,8]{0,1:T(8,128)}, u32[]{:S(2)}) copy-start(s32[64,8]{0,1:T(8,128)} %param.8) | copy-start | bytes 6148
  263.0 52.1 %all-to-all-start.3 = ((bf16[16,16,3,2048]{3,1,2,0:T(8,128)(2,1)}), bf16[16,16,3,2048]{3,1,2,0:T(8,128)(2,1)S(1)}, u32[]{:S(2)}, u32[]{:S(2)}) async-start(bf16[16,16,3,2048]{3,1,2,0:T(8,128)(2,1)} %copy.23), calls=%async_computation.3 | async-start | bytes 6291456 | tf_op jit(solution)/shard_map/all_to_all | solution.py:53
  327.4 7.6 %copy-start.1 = (bf16[64,2048]{1,0:T(8,128)(2,1)S(1)}, bf16[64,2048]{1,0:T(8,128)(2,1)}, u32[]{:S(2)}) copy-start(bf16[64,2048]{1,0:T(8,128)(2,1)} %param.6) | copy-start | bytes 786436
where the time goes:
time: 336 us; the launch traced here: 335 us
  blocking collectives  125 us (37%)
  waiting for transfers between devices  118 us (35%)
  local copies, waits for them, and re-layouts  58.7 us (17%)
  starting transfers between devices  15.3 us (5%)
  matrix products  12.8 us (4%)
  other arithmetic  5.1 us (2%)
    all_to_all x1, blocking collectives, per_device(): lax.all_to_all(expert_out.reshape(shape_in), 'expert', split_axis=1, conc...  78.7 us
    all_to_all x1, waiting for transfers between devices, per_device(): lax.all_to_all(first_section, 'expert', split_axis=1, concat_axis=1, tile...  70.3 us
    all_to_all x1, waiting for transfers between devices, per_device(): lax.all_to_all(returned, 'dp', split_axis=0, concat_axis=0, tiled=True)  47.9 us
    all_to_all x1, blocking collectives, per_device(): lax.all_to_all(outgoing, 'dp', split_axis=0, concat_axis=0, tiled=True)  46 us
    all_to_all x1, starting transfers between devices, per_device(): lax.all_to_all(first_section, 'expert', split_axis=1, concat_axis=1, tile...  10.5 us
    reshape x2, local copies, waits for them, and re-layouts, per_device(): expert_out.reshape(shape_in)  9.13 us
    reshape x2, local copies, waits for them, and re-layouts, per_device(): outgoing = outgoing.reshape(dp_count, col_count, capacity, width)  9.13 us
    reshape x1, local copies, waits for them, and re-layouts, per_device(): token_rows = arrived.reshape(-1, width)  7.51 us
  transfers between devices with their start and end apart: 5, of which 2 were waited for; matrix products, arithmetic and copies ran while one was open for 6% of the time, Pallas kernels for 0%

commit v1 on v0

--- a/solution.py
+++ b/solution.py
@@ -47,8 +47,16 @@
     up_part = jnp.dot(token_rows, up_full, preferred_element_type=jnp.float32)
     hidden = (jax.nn.silu(gate_part) * up_part).astype(jnp.bfloat16)
     expert_out = jnp.dot(hidden, down_full, preferred_element_type=jnp.float32).astype(jnp.bfloat16)
-    returned = lax.all_to_all(
-        expert_out.reshape(shape_in), "expert", split_axis=1, concat_axis=1, tiled=True
+    returned = jnp.concatenate(
+        lax.all_to_all(
+            jnp.stack(
+                jnp.split(expert_out.reshape(shape_in), lax.axis_size("expert"), axis=1), axis=0
+            ),
+            "expert",
+            0,
+            0,
+        ),
+        axis=1,
     )
     home = lax.all_to_all(returned, "dp", split_axis=0, concat_axis=0, tiled=True)
     home_flat = home.reshape(dev_count * capacity, width)

time: 336 us -> 351 us (1.045)
  local copies, waits for them, and re-layouts: 58.7 us -> 73.7 us
    unnamed x12 -> x27, local copies, waits for them, and re-layouts: 0.85 us -> 16.9 us
    reshape x2 -> x1, local copies, waits for them, and re-layouts: 9.13 us -> 4.43 us  [per_device(): expert_out.reshape(shape_in)]
    another operation x3 -> x5, local copies, waits for them, and re-layouts: 0.03 us -> 3.62 us  [the longest x2 3.59 us: per_device(): jnp.stack(jnp.split(expert_out.reshape(shape_in), lax.axis_size('expert')...]
where the time goes in v1:
time: 351 us; the launch traced here: 350 us
  blocking collectives  125 us (36%)
  waiting for transfers between devices  118 us (34%)
  local copies, waits for them, and re-layouts  73.7 us (21%)
  starting transfers between devices  15 us (4%)
  matrix products  12.8 us (4%)
  other arithmetic  5.1 us (1%)
    all_to_all x1, blocking collectives, per_device(): lax.all_to_all(jnp.stack(jnp.split(expert_out.reshape(shape_in), lax.axis...  78.7 us
    all_to_all x1, waiting for transfers between devices, per_device(): lax.all_to_all(first_section, 'expert', split_axis=1, concat_axis=1, tile...  70.3 us
    all_to_all x1, waiting for transfers between devices, per_device(): lax.all_to_all(returned, 'dp', split_axis=0, concat_axis=0, tiled=True)  48.1 us
    all_to_all x1, blocking collectives, per_device(): lax.all_to_all(outgoing, 'dp', split_axis=0, concat_axis=0, tiled=True)  46 us
    unnamed x27, local copies, waits for them, and re-layouts  16.9 us
    all_to_all x1, starting transfers between devices, per_device(): lax.all_to_all(first_section, 'expert', split_axis=1, concat_axis=1, tile...  10.5 us
    reshape x2, local copies, waits for them, and re-layouts, per_device(): outgoing = outgoing.reshape(dp_count, col_count, capacity, width)  9.13 us
    reshape x1, local copies, waits for them, and re-layouts, per_device(): token_rows = arrived.reshape(-1, width)  7.51 us
  transfers between devices with their start and end apart: 5, of which 2 were waited for; matrix products, arithmetic and copies ran while one was open for 6% of the time, Pallas kernels for 0%

profile of v1, /device:TPU:1, one launch (start us, length us, event | category | flops | bytes accessed | tf_op | source)
XLA Modules:
  0.0 350.1 jit_solution(1185155154330522591)
XLA Ops:
  2.2 4.6 %scatter_custom_fusion = bf16[768,2048]{1,0:T(8,128)(2,1)S(1)} fusion(s32[512]{0:T(512)S(1)} %bitcast.125, bf16[]{:T(256)} %constant.54.clone.1, bf16[64,2048]{1,0:T(8,128)(2,1)S(1)} %copy-done), kind=kCustom, calls=%fused_computation.17 | custom fusion | bytes 3407874 | tf_op jit(solution)/shard_map/scatter | solution.py:40
  6.8 4.4 %reshape.265 = bf16[16,16,3,2048]{3,2,1,0:T(4,128)(2,1)} reshape(bf16[768,2048]{1,0:T(8,128)(2,1)S(1)} %scatter_custom_fusion) | data formatting | bytes 6291456 | tf_op jit(solution)/shard_map/reshape | solution.py:41
  11.2 4.7 %copy.51 = bf16[16,16,3,2048]{3,1,2,0:T(8,128)(2,1)S(1)} copy(bf16[16,16,3,2048]{3,2,1,0:T(4,128)(2,1)} %reshape.265) | data formatting | bytes 6291456 | tf_op jit(solution)/shard_map/reshape | solution.py:41
  15.9 46.0 %all_to_all.20 = bf16[16,16,3,2048]{3,1,2,0:T(8,128)(2,1)S(1)} all-to-all(bf16[16,16,3,2048]{3,1,2,0:T(8,128)(2,1)S(1)} %copy.51), channel_id=1, replica_groups=mesh['dp'=16,'expert'=16] {'dp'}, dimensions={0} | all-to-all | bytes 6291456 | tf_op jit(solution)/shard_map/all_to_all | solution.py:42
  61.9 3.4 copy.52
  65.3 10.5 %all-to-all-start.1 = ((bf16[16,16,3,2048]{3,0,2,1:T(8,128)(2,1)}), bf16[16,16,3,2048]{3,0,2,1:T(8,128)(2,1)S(1)}, u32[]{:S(2)}, u32[]{:S(2)}) async-start(bf16[16,16,3,2048]{3,0,2,1:T(8,128)(2,1)} %copy.52), calls=%async_computation.1 | async-start | bytes 6291456 | tf_op jit(solution)/shard_map/all_to_all | solution.py:43
  76.5 70.3 %all-to-all-done.1 = bf16[16,16,3,2048]{3,0,2,1:T(8,128)(2,1)S(1)} async-done(((bf16[16,16,3,2048]{3,0,2,1:T(8,128)(2,1)}), bf16[16,16,3,2048]{3,0,2,1:T(8,128)(2,1)S(1)}, u32[]{:S(2)}, u32[]{:S(2)}) %all-to-all-start.1) | async-done | bytes 3145760 | tf_op jit(solution)/shard_map/all_to_all | solution.py:43
  146.8 4.6 %copy.53 = bf16[16,16,3,2048]{3,2,1,0:T(4,128)(2,1)} copy(bf16[16,16,3,2048]{3,0,2,1:T(8,128)(2,1)S(1)} %all-to-all-done.1) | data formatting | bytes 6291456 | tf_op jit(solution)/shard_map/all_to_all | solution.py:43
  151.4 7.5 %reshape.266 = bf16[768,2048]{1,0:T(8,128)(2,1)S(1)} reshape(bf16[16,16,3,2048]{3,2,1,0:T(4,128)(2,1)} %copy.53) | data formatting | bytes 6291456 | tf_op jit(solution)/shard_map/reshape | solution.py:45
  158.9 4.6 %fusion.1 = f32[768,768]{1,0:T(8,128)S(1)} fusion(bf16[768,2048]{1,0:T(8,128)(2,1)S(1)} %reshape.266, bf16[2048,384]{1,0:T(8,128)(2,1)} %collective-permute-done, bf16[2048,384]{1,0:T(8,128)(2,1)} %bitcast.129), kind=kOutput, calls=%fused_computation.5 | convolution fusion | flops 2422210560 | bytes 8650752 | tf_op jit(solution)/shard_map/dot_general | solution.py:46
  163.5 4.1 %fusion.5 = f32[768,768]{1,0:T(8,128)S(1)} fusion(bf16[768,2048]{1,0:T(8,128)(2,1)S(1)} %reshape.266, bf16[2048,384]{1,0:T(8,128)(2,1)} %collective-permute-done.1, bf16[2048,384]{1,0:T(8,128)(2,1)S(1)} %bitcast.131), kind=kOutput, calls=%fused_computation.9 | convolution fusion | flops 2422210560 | bytes 8650752 | tf_op jit(solution)/shard_map/dot_general | solution.py:47
  167.7 4.1 %convolution_convert_fusion = bf16[768,2048]{1,0:T(8,128)(2,1)S(1)} fusion(bf16[384,2048]{1,0:T(8,128)(2,1)} %collective-permute-done.2, bf16[384,2048]{1,0:T(8,128)(2,1)S(1)} %bitcast.133, f32[768,768]{1,0:T(8,128)S(1)} %fusion.5, f32[768,768]{1,0:T(8,128)S(1)} %fusion.1), kind=kOutput, calls=%fused_computation.4 | convolution fusion | flops 2427322368 | bytes 11010048 | tf_op jit(solution)/shard_map/dot_general | solution.py:49
  171.8 4.4 %reshape.267 = bf16[16,16,3,2048]{3,2,1,0:T(4,128)(2,1)} reshape(bf16[768,2048]{1,0:T(8,128)(2,1)S(1)} %convolution_convert_fusion) | data formatting | bytes 6291456 | tf_op jit(solution)/shard_map/reshape | solution.py:53
  178.3 1.1 fusion.31
  179.4 1.1 fusion.30
  193.5 2.5 copy.69
  196.0 78.7 %all_to_all.21 = bf16[16,16,1,3,2048]{4,1,3,2,0:T(8,128)(2,1)S(1)} all-to-all(bf16[16,16,1,3,2048]{4,1,3,2,0:T(8,128)(2,1)S(1)} %copy.69), channel_id=1, replica_groups=mesh['dp'=16,'expert'=16] {'expert'}, dimensions={0} | all-to-all | bytes 6291456 | tf_op jit(solution)/shard_map/all_to_all | solution.py:51
  274.8 3.4 copy.70
  278.1 3.9 %all-to-all-start.3 = ((bf16[16,16,3,2048]{3,1,2,0:T(8,128)(2,1)}), bf16[16,16,3,2048]{3,1,2,0:T(8,128)(2,1)S(1)}, u32[]{:S(2)}, u32[]{:S(2)}) async-start(bf16[16,16,3,2048]{3,1,2,0:T(8,128)(2,1)} %copy.70), calls=%async_computation.3 | async-start | bytes 6291456 | tf_op jit(solution)/shard_map/all_to_all | solution.py:61
  282.2 48.1 %all-to-all-done.3 = bf16[16,16,3,2048]{3,1,2,0:T(8,128)(2,1)S(1)} async-done(((bf16[16,16,3,2048]{3,1,2,0:T(8,128)(2,1)}), bf16[16,16,3,2048]{3,1,2,0:T(8,128)(2,1)S(1)}, u32[]{:S(2)}, u32[]{:S(2)}) %all-to-all-start.3) | async-done | bytes 3145760 | tf_op jit(solution)/shard_map/all_to_all | solution.py:61
  330.3 4.7 %copy.71 = bf16[16,16,3,2048]{3,2,1,0:T(4,128)(2,1)} copy(bf16[16,16,3,2048]{3,1,2,0:T(8,128)(2,1)S(1)} %all-to-all-done.3) | data formatting | bytes 6291456 | tf_op jit(solution)/shard_map/all_to_all | solution.py:61
  335.0 7.5 %reshape.270 = bf16[768,2048]{1,0:T(8,128)(2,1)S(1)} reshape(bf16[16,16,3,2048]{3,2,1,0:T(4,128)(2,1)} %copy.71) | data formatting | bytes 6291456 | tf_op jit(solution)/shard_map/reshape | solution.py:62
  342.5 3.3 gather_fusion
  345.8 4.2 %fusion = f32[64,2048]{1,0:T(8,128)} fusion(bf16[512,2048]{1,0:T(8,128)(2,1)} %gather_fusion, f32[64,8]{1,0:T(8,128)S(1)} %copy.72), kind=kLoop, calls=%fused_computation.3 | loop fusion | flops 3014656 | bytes 2623488 | tf_op jit(solution)/shard_map/reduce_sum | solution.py:64
  (48 shorter events, 18.0 us)
Async XLA Ops:
  0.0 2.2 copy-start
  65.3 81.4 %all-to-all-start.1 = ((bf16[16,16,3,2048]{3,0,2,1:T(8,128)(2,1)}), bf16[16,16,3,2048]{3,0,2,1:T(8,128)(2,1)S(1)}, u32[]{:S(2)}, u32[]{:S(2)}) async-start(bf16[16,16,3,2048]{3,0,2,1:T(8,128)(2,1)} %copy.52), calls=%async_computation.1 | async-start | bytes 6291456 | tf_op jit(solution)/shard_map/all_to_all | solution.py:43
  75.8 83.1 %collective-permute-start = (bf16[2048,384]{1,0:T(8,128)(2,1)}, bf16[2048,384]{1,0:T(8,128)(2,1)}, u32[]{:S(2)}, u32[]{:S(2)}) collective-permute-start(bf16[2048,384]{1,0:T(8,128)(2,1)} %bitcast.128), channel_id=1, source_target_pairs={{0,1},{1,0},{2,3},{3,2},{4,5},{5,4},{6,7},{7,6},{8,9},{9,8},{10,11... | collective-permute-start | bytes 4718600 | tf_op jit(solution)/shard_map/ppermute | solution.py:8
  76.0 87.6 %collective-permute-start.1 = (bf16[2048,384]{1,0:T(8,128)(2,1)}, bf16[2048,384]{1,0:T(8,128)(2,1)}, u32[]{:S(2)}, u32[]{:S(2)}) collective-permute-start(bf16[2048,384]{1,0:T(8,128)(2,1)} %bitcast.130), channel_id=1, source_target_pairs={{0,1},{1,0},{2,3},{3,2},{4,5},{5,4},{6,7},{7,6},{8,9},{9,8},{10,11... | collective-permute-start | bytes 4718600 | tf_op jit(solution)/shard_map/ppermute | solution.py:8
  76.3 91.4 %collective-permute-start.2 = (bf16[384,2048]{1,0:T(8,128)(2,1)}, bf16[384,2048]{1,0:T(8,128)(2,1)}, u32[]{:S(2)}, u32[]{:S(2)}) collective-permute-start(bf16[384,2048]{1,0:T(8,128)(2,1)} %bitcast.132), channel_id=1, source_target_pairs={{0,1},{1,0},{2,3},{3,2},{4,5},{5,4},{6,7},{7,6},{8,9},{9,8},{10,11... | collective-permute-start | bytes 4718600 | tf_op jit(solution)/shard_map/ppermute | solution.py:8
  158.9 4.6 %copy-start.3 = (bf16[1,2048,384]{2,1,0:T(8,128)(2,1)S(1)}, bf16[1,2048,384]{2,1,0:T(8,128)(2,1)}, u32[]{:S(2)}) copy-start(bf16[1,2048,384]{2,1,0:T(8,128)(2,1)} %param.10) | copy-start | bytes 4718596
  163.5 4.2 %copy-start.4 = (bf16[1,384,2048]{2,1,0:T(8,128)(2,1)S(1)}, bf16[1,384,2048]{2,1,0:T(8,128)(2,1)}, u32[]{:S(2)}) copy-start(bf16[1,384,2048]{2,1,0:T(8,128)(2,1)} %param.11) | copy-start | bytes 4718596
  278.1 3.9 %copy-start.2 = (s32[64,8]{0,1:T(8,128)S(1)}, s32[64,8]{0,1:T(8,128)}, u32[]{:S(2)}) copy-start(s32[64,8]{0,1:T(8,128)} %param.8) | copy-start | bytes 6148
  278.1 52.1 %all-to-all-start.3 = ((bf16[16,16,3,2048]{3,1,2,0:T(8,128)(2,1)}), bf16[16,16,3,2048]{3,1,2,0:T(8,128)(2,1)S(1)}, u32[]{:S(2)}, u32[]{:S(2)}) async-start(bf16[16,16,3,2048]{3,1,2,0:T(8,128)(2,1)} %copy.70), calls=%async_computation.3 | async-start | bytes 6291456 | tf_op jit(solution)/shard_map/all_to_all | solution.py:61
  342.5 7.6 %copy-start.1 = (bf16[64,2048]{1,0:T(8,128)(2,1)S(1)}, bf16[64,2048]{1,0:T(8,128)(2,1)}, u32[]{:S(2)}) copy-start(bf16[64,2048]{1,0:T(8,128)(2,1)} %param.6) | copy-start | bytes 786436
